TPU v7x, 128 devices: a whole 4x4x4 slice. The times are simulated.
128 devices in a mesh: section: 4 (over y), seq: 32 (over z, x, core).
Axes of the slice: x: 4, y: 4, z: 4, core: 2. Of those that a mesh axis runs over, the one named last changes fastest.
Arguments:
- layer_input: bfloat16 [4, 2, 2048, 8192], P('section', None, 'seq'), may hold values from -60 to 60
- query_act: bfloat16 [4, 2, 2048, 8192], P('section', None, 'seq'), may hold values from -8 to 8
- key_act: bfloat16 [4, 2, 2048, 1024], P('section', None, 'seq'), may hold values from -6 to 6
- value_act: bfloat16 [4, 2, 2048, 1024], P('section', None, 'seq'), may hold values from -6 to 6
- output_grad: bfloat16 [4, 2, 2048, 8192], P('section', None, 'seq'), may hold values from -24 to 24
- value_weight: bfloat16 [4, 8192, 1024], P('section', 'seq'), may hold values from -0.0625 to 0.0625
- norm_gain: float32 [4, 8192], P('section'), may hold values from 0.1 to 1.9
- top_grad: bfloat16 [2, 2048, 8192], P(None, 'seq'), may hold values from -3 to 3
Outputs:
- input_grad: bfloat16 [4, 2, 2048, 8192], P('section', None, 'seq')
- query_grad: bfloat16 [4, 2, 2048, 8192], P('section', None, 'seq')
- key_grad: bfloat16 [4, 2, 2048, 1024], P('section', None, 'seq')
All inputs are finite; a program needn't handle non-finite values.
Results may differ from a plain program's by a relative error of at most 0.015.
Values may be sent and summed in bfloat16 or wider, within the bound.
No kernel may reach another device: no remote copies, remote signals or barrier semaphores. Data moves between devices by JAX's collectives and lax.ppermute only.
A program may use at most 192 MiB of HBM per device.

v0:
```python
import jax
import jax.numpy as jnp
from jax import lax
from jax.experimental import pallas as pl
from jax.experimental.pallas import tpu as pltpu
from jax.sharding import PartitionSpec as P

D = 8192
KV_HEADS = 8
HEAD_DIM = 128
BATCH = 2
SEQ = 2048
DEVICES = 32
LOCAL = SEQ // DEVICES
UNIT_HEADS = 4
QCOLS = UNIT_HEADS * HEAD_DIM
UNITS = DEVICES // BATCH
PACK = QCOLS + HEAD_DIM
STEP_UNITS = 8
TOK = 128
BLOCKS = SEQ // TOK
CHUNK = 256
CHUNKS = SEQ // CHUNK
HALF = BLOCKS // 2
SIDES = 2
STEPS = BLOCKS // SIDES
HALF_CHUNKS = CHUNKS // 2
SCALE = HEAD_DIM ** (-0.5)
LOG2E = 1.4426950408889634
NEG = -1e30

BF = jnp.bfloat16
F32 = jnp.float32
LAST = (((1,), (1,)), ((), ()))


PARAMS = pltpu.CompilerParams(vmem_limit_bytes=60 << 20)


def cost(us):
    return pl.CostEstimate(flops=int(us * 1e9), transcendentals=0, bytes_accessed=0)


def pack_body(q_ref, g_ref, k_ref, v_ref, out_ref):
    for unit in range(STEP_UNITS):
        cols = slice(unit * QCOLS, (unit + 1) * QCOLS)
        kv = slice(unit // 2 * HEAD_DIM, (unit // 2 + 1) * HEAD_DIM)
        out_ref[unit, :, :QCOLS] = q_ref[:, cols]
        out_ref[unit, :, QCOLS : 2 * QCOLS] = g_ref[:, cols]
        out_ref[unit, :, 2 * QCOLS : 2 * QCOLS + HEAD_DIM] = k_ref[:, kv]
        out_ref[unit, :, 2 * QCOLS + HEAD_DIM :] = v_ref[:, kv]


def pack(q, g, k, v):
    wide = pl.BlockSpec((None, LOCAL, STEP_UNITS * QCOLS), lambda b, i: (b, 0, i))
    slim = pl.BlockSpec((None, LOCAL, STEP_UNITS // 2 * HEAD_DIM), lambda b, i: (b, 0, i))
    per_seq = UNITS // STEP_UNITS
    return pl.pallas_call(
        pack_body,
        grid=(BATCH, per_seq),
        out_shape=jax.ShapeDtypeStruct((DEVICES, LOCAL, 2 * PACK), BF),
        in_specs=[wide, wide, slim, slim],
        out_specs=pl.BlockSpec(
            (STEP_UNITS, LOCAL, 2 * PACK), lambda b, i: (b * per_seq + i, 0, 0)
        ),
        compiler_params=PARAMS,
        cost_estimate=cost(6),
        name="pack",
    )(q, g, k, v)


def unpack_body(in_ref, wide_ref, slim_ref):
    for unit in range(STEP_UNITS):
        wide_ref[:, unit * QCOLS : (unit + 1) * QCOLS] = in_ref[unit, :, :QCOLS]
    for head in range(STEP_UNITS // 2):
        total = in_ref[2 * head, :, QCOLS:].astype(F32) + in_ref[2 * head + 1, :, QCOLS:].astype(F32)
        slim_ref[:, head * HEAD_DIM : (head + 1) * HEAD_DIM] = total.astype(BF)


def unpack(parts):
    per_seq = UNITS // STEP_UNITS
    return pl.pallas_call(
        unpack_body,
        grid=(BATCH, per_seq),
        out_shape=(
            jax.ShapeDtypeStruct((BATCH, LOCAL, D), BF),
            jax.ShapeDtypeStruct((BATCH, LOCAL, KV_HEADS * HEAD_DIM), BF),
        ),
        in_specs=[pl.BlockSpec((STEP_UNITS, LOCAL, PACK), lambda b, i: (b * per_seq + i, 0, 0))],
        out_specs=(
            pl.BlockSpec((None, LOCAL, STEP_UNITS * QCOLS), lambda b, i: (b, 0, i)),
            pl.BlockSpec((None, LOCAL, STEP_UNITS // 2 * HEAD_DIM), lambda b, i: (b, 0, i)),
        ),
        cost_estimate=cost(5),
        compiler_params=PARAMS,
        name="unpack",
    )(parts)


def stack_heads(ref, side):
    rows = pl.ds(pl.multiple_of(side * TOK, TOK), TOK)
    return jnp.concatenate(
        [ref[rows, h * HEAD_DIM : (h + 1) * HEAD_DIM] for h in range(UNIT_HEADS)], axis=0
    )


def fold(chunk, op):
    return op(chunk.reshape(CHUNK // 8, 8, QCOLS), axis=0)


def join(a, b, op):
    return b if a is None else op(a, b)


def chunk_rows(c):
    return slice(c * CHUNK, (c + 1) * CHUNK)


def score_chunk(q, k_ref, s_ref, block, last, top, c):
    s = lax.dot_general(k_ref[chunk_rows(c), :], q, LAST, preferred_element_type=F32)
    if c == last:
        key_pos = c * CHUNK + lax.broadcasted_iota(jnp.int32, (CHUNK, QCOLS), 0)
        query_pos = block * TOK + lax.broadcasted_iota(jnp.int32, (CHUNK, QCOLS), 1) % TOK
        s = jnp.where(key_pos <= query_pos, s, NEG)
    s_ref[c] = s
    return join(top, fold(s, jnp.max), jnp.maximum)


def scaled_grad(g, inverse):
    column = jnp.transpose(jnp.broadcast_to(inverse, (HEAD_DIM, QCOLS)))
    return (g.astype(F32) * column).astype(BF)


def probs_body(q_ref, g_ref, k_ref, low_ref, high_ref, l_ref, dv_ref, s_ref, acc):
    step = pl.program_id(0)

    @pl.when(step == 0)
    def _():
        acc[...] = jnp.zeros_like(acc)

    for last in range(CHUNKS):
        e_ref = low_ref if last < HALF_CHUNKS else high_ref

        @pl.when(step * SIDES // 2 == last)
        def _():
            def one_block(side, carry):
                q = stack_heads(q_ref, side)
                top = None
                for c in range(last + 1):
                    top = score_chunk(q, k_ref, s_ref, step * SIDES + side, last, top, c)
                top = jnp.max(top, axis=0, keepdims=True)
                total = None
                for c in range(last + 1):
                    e = jnp.exp2((s_ref[c] - top) * (SCALE * LOG2E))
                    e_ref[side, c] = e.astype(BF)
                    total = join(total, fold(e, jnp.sum), jnp.add)
                inverse = 1.0 / jnp.sum(total, axis=0, keepdims=True)
                l_ref[side] = inverse
                g = scaled_grad(stack_heads(g_ref, side), inverse)
                for c in range(last + 1):
                    acc[chunk_rows(c), :] += jnp.dot(
                        e_ref[side, c], g, preferred_element_type=F32
                    )
                return carry

            lax.fori_loop(0, SIDES, one_block, 0)

    @pl.when(step == STEPS - 1)
    def _():
        dv_ref[...] = acc[...].astype(BF)


LOW_SPEC = pl.BlockSpec(
    (SIDES, HALF_CHUNKS, CHUNK, QCOLS), lambda t: (jnp.minimum(t, STEPS // 2 - 1), 0, 0, 0)
)
HIGH_SPEC = pl.BlockSpec(
    (SIDES, CHUNKS, CHUNK, QCOLS), lambda t: (jnp.maximum(t - STEPS // 2, 0), 0, 0, 0)
)
STAT_SPEC = pl.BlockSpec((SIDES, 1, QCOLS), lambda t: (t, 0, 0))
Q_SPEC = pl.BlockSpec((SIDES * TOK, QCOLS), lambda t: (t, 0))
G_SPEC = pl.BlockSpec((SIDES * TOK, QCOLS), lambda t: (t, 1))
K_SPEC = pl.BlockSpec((SEQ, HEAD_DIM), lambda t: (0, 2 * UNIT_HEADS))
V_SPEC = pl.BlockSpec((SEQ, HEAD_DIM), lambda t: (0, 2 * UNIT_HEADS + 1))


def attend_probs(packed):
    return pl.pallas_call(
        probs_body,
        grid=(STEPS,),
        out_shape=(
            jax.ShapeDtypeStruct((HALF, HALF_CHUNKS, CHUNK, QCOLS), BF),
            jax.ShapeDtypeStruct((HALF, CHUNKS, CHUNK, QCOLS), BF),
            jax.ShapeDtypeStruct((BLOCKS, 1, QCOLS), F32),
            jax.ShapeDtypeStruct((SEQ, HEAD_DIM), BF),
        ),
        in_specs=[Q_SPEC, G_SPEC, K_SPEC],
        out_specs=(
            LOW_SPEC,
            HIGH_SPEC,
            STAT_SPEC,
            pl.BlockSpec((SEQ, HEAD_DIM), lambda t: (0, 0)),
        ),
        scratch_shapes=[
            pltpu.VMEM((CHUNKS, CHUNK, QCOLS), F32),
            pltpu.VMEM((SEQ, HEAD_DIM), F32),
        ],
        compiler_params=PARAMS,
        cost_estimate=cost(27),
        name="probs",
    )(packed, packed, packed)


def grads_body(
    q_ref, g_ref, k_ref, v_ref, low_ref, high_ref, l_ref, out_ref, p_ref, kt_ref, acc
):
    step = pl.program_id(0)
    place = STEPS - 1 - step

    @pl.when(step == 0)
    def _():
        acc[...] = jnp.zeros_like(acc)
        for c in range(CHUNKS):
            kt_ref[c] = jnp.transpose(k_ref[chunk_rows(c), :])

    for last in range(CHUNKS):
        e_ref = low_ref if last < HALF_CHUNKS else high_ref

        @pl.when(place * SIDES // 2 == last)
        def _():
            def one_block(side, carry):
                inverse = l_ref[side]
                g = scaled_grad(stack_heads(g_ref, side), inverse)
                total = None
                for c in range(last + 1):
                    p = lax.dot_general(
                        v_ref[chunk_rows(c), :], g, LAST, preferred_element_type=F32
                    )
                    p_ref[c] = p
                    total = join(total, fold(p * e_ref[side, c].astype(F32), jnp.sum), jnp.add)
                center = jnp.sum(total, axis=0, keepdims=True) * inverse
                q = stack_heads(q_ref, side)
                dq = None
                for c in range(last + 1):
                    ds = (e_ref[side, c].astype(F32) * (p_ref[c] - center)).astype(BF)
                    acc[chunk_rows(c), :] += jnp.dot(ds, q, preferred_element_type=F32)
                    dq = join(dq, jnp.dot(kt_ref[c], ds, preferred_element_type=F32), jnp.add)
                dq = dq * SCALE
                rows = pl.ds(pl.multiple_of(side * TOK, TOK), TOK)
                for h in range(UNIT_HEADS):
                    cols = slice(h * HEAD_DIM, (h + 1) * HEAD_DIM)
                    out_ref[rows, cols] = jnp.transpose(dq[:, cols]).astype(BF)
                return carry

            lax.fori_loop(0, SIDES, one_block, 0)

    rows = pl.ds(pl.multiple_of(place * SIDES * TOK, SIDES * TOK), SIDES * TOK)
    out_ref[:, QCOLS:] = (acc[rows, :] * SCALE).astype(BF)


def backward(spec):
    index = spec.index_map
    return pl.BlockSpec(spec.block_shape, lambda t: index(STEPS - 1 - t))


def attend_grads(packed, low, high, inverse):
    return pl.pallas_call(
        grads_body,
        grid=(STEPS,),
        out_shape=jax.ShapeDtypeStruct((SEQ, PACK), BF),
        in_specs=[backward(Q_SPEC), backward(G_SPEC), K_SPEC, V_SPEC]
        + [backward(LOW_SPEC), backward(HIGH_SPEC), backward(STAT_SPEC)],
        out_specs=backward(pl.BlockSpec((SIDES * TOK, PACK), lambda t: (t, 0))),
        scratch_shapes=[
            pltpu.VMEM((CHUNKS, CHUNK, QCOLS), F32),
            pltpu.VMEM((CHUNKS, HEAD_DIM, CHUNK), BF),
            pltpu.VMEM((SEQ, HEAD_DIM), F32),
        ],
        compiler_params=PARAMS,
        cost_estimate=cost(27),
        name="grads",
    )(packed, packed, packed, packed, low, high, inverse)


ROWS = BATCH * LOCAL
FEATS = D // DEVICES
PIECES = 8
SECTIONS = 4
HALVES = 2
PART = ROWS // SECTIONS // HALVES


def pair_sums(parts_ref, emit):
    for seq in range(BATCH):
        for head in range(KV_HEADS):
            first = seq * UNITS + 2 * head
            total = parts_ref[first].astype(F32) + parts_ref[first + 1].astype(F32)
            emit(seq, slice(head * HEAD_DIM, (head + 1) * HEAD_DIM), total.astype(BF))


def term_body(here_ref, parts_ref, w_ref, x_ref, gain_ref, top_ref, *refs):
    out_refs, (vg_ref, u_ref, xs_ref, acc) = refs[:-4], refs[-4:]
    step = pl.program_id(0)
    here = here_ref[0]

    @pl.when(step == 0)
    def _():
        acc[...] = jnp.zeros_like(acc)

        def emit(seq, cols, value):
            vg_ref[seq * LOCAL : (seq + 1) * LOCAL, cols] = value

        pair_sums(parts_ref, emit)

    dots = lax.dot_general(vg_ref[...], w_ref[...], LAST, preferred_element_type=F32)
    squares = jnp.zeros((ROWS, 1), F32)
    inner = jnp.zeros((ROWS, 1), F32)
    for i in range(PIECES):
        cols = slice(i * FEATS, (i + 1) * FEATS)
        x = x_ref[:, cols].astype(F32)
        u = dots[:, cols] * gain_ref[:, cols]
        u_ref[step * PIECES + i] = u
        xs_ref[step * PIECES + i] = x_ref[:, cols]
        squares = squares + jnp.sum(x * x, axis=1, keepdims=True)
        inner = inner + jnp.sum(x * u, axis=1, keepdims=True)
    acc[0] += squares
    acc[1] += inner

    @pl.when(step == pl.num_programs(0) - 1)
    def _():
        flag = jnp.where(here == SECTIONS - 1, 1.0, 0.0).astype(F32)
        r = lax.rsqrt(acc[0] * (1.0 / D) + 1e-05)
        acc[1] = acc[1] * (1.0 / D) * (r * r * r)
        acc[0] = r
        for half in range(HALVES * SECTIONS):
            first = ((here + half % SECTIONS) % SECTIONS * HALVES + half // SECTIONS) * PART
            rows = pl.ds(pl.multiple_of(first, PART), PART)
            r = acc[0, rows, :]
            inner = acc[1, rows, :]

            def finish(i, carry):
                cols = pl.ds(pl.multiple_of(i * FEATS, FEATS), FEATS)
                term = r * u_ref[i, rows, :] - xs_ref[i, rows, :].astype(F32) * inner
                term = term + top_ref[rows, cols].astype(F32) * flag
                out_refs[half][:, cols] = term.astype(BF)
                return carry

            lax.fori_loop(0, D // FEATS, finish, 0, unroll=4)


def norm_term(here, parts, weight, x, gain, top):
    width = PIECES * FEATS
    return pl.pallas_call(
        term_body,
        grid=(D // width,),
        out_shape=(jax.ShapeDtypeStruct((PART, D), BF),) * (HALVES * SECTIONS),
        in_specs=[
            pl.BlockSpec(memory_space=pltpu.SMEM),
            pl.BlockSpec((DEVICES, LOCAL, HEAD_DIM), lambda i: (0, 0, 0)),
            pl.BlockSpec((width, KV_HEADS * HEAD_DIM), lambda i: (i, 0)),
            pl.BlockSpec((ROWS, width), lambda i: (0, i)),
            pl.BlockSpec((1, width), lambda i: (0, i)),
            pl.BlockSpec((ROWS, D), lambda i: (0, 0)),
        ],
        out_specs=(pl.BlockSpec((PART, D), lambda i: (0, 0)),) * (HALVES * SECTIONS),
        scratch_shapes=[
            pltpu.VMEM((ROWS, KV_HEADS * HEAD_DIM), BF),
            pltpu.VMEM((D // FEATS, ROWS, FEATS), F32),
            pltpu.VMEM((D // FEATS, ROWS, FEATS), BF),
            pltpu.VMEM((2, ROWS, 1), F32),
        ],
        compiler_params=PARAMS,
        cost_estimate=cost(12),
        name="term",
    )(here, parts, weight, x, gain, top)


def sums_body(here_ref, *refs):
    parts, outs = refs[:SECTIONS], refs[SECTIONS:]
    here = here_ref[0]
    place = [(here - j) % SECTIONS for j in range(SECTIONS)]
    values = [part[...].astype(F32) for part in parts]
    for k in range(SECTIONS):
        total = values[k]
        for j in range(SECTIONS):
            if j != k:
                total = total + values[j] * jnp.where(place[j] > place[k], 1.0, 0.0).astype(F32)
        outs[k][...] = total.astype(BF)


def suffix_sums(here, parts):
    cols = D // 2
    spec = pl.BlockSpec((PART, cols), lambda i: (0, i))
    return pl.pallas_call(
        sums_body,
        grid=(D // cols,),
        out_shape=tuple(jax.ShapeDtypeStruct((PART, D), BF) for _ in range(SECTIONS)),
        in_specs=[pl.BlockSpec(memory_space=pltpu.SMEM)] + [spec] * SECTIONS,
        out_specs=(spec,) * SECTIONS,
        cost_estimate=cost(2),
        compiler_params=PARAMS,
        name="suffix_sums",
    )(here, *parts)


def place_body(here_ref, *refs):
    parts, out_ref = refs[:-1], refs[-1]
    here = here_ref[0]
    for half in range(HALVES * SECTIONS):
        first = ((here + half % SECTIONS) % SECTIONS * HALVES + half // SECTIONS) * PART
        rows = pl.ds(pl.multiple_of(first, PART), PART)
        out_ref[rows, :] = parts[half][...]


def place(here, parts):
    cols = D // 2
    spec = pl.BlockSpec((PART, cols), lambda i: (0, i))
    return pl.pallas_call(
        place_body,
        grid=(D // cols,),
        out_shape=jax.ShapeDtypeStruct((ROWS, D), BF),
        in_specs=[pl.BlockSpec(memory_space=pltpu.SMEM)] + [spec] * (HALVES * SECTIONS),
        out_specs=pl.BlockSpec((ROWS, cols), lambda i: (0, i)),
        cost_estimate=cost(2),
        compiler_params=PARAMS,
        name="place",
    )(here, *parts)


def exchange(parts):
    return lax.all_to_all(parts, "seq", 0, 0, tiled=True)


def turn(array, by):
    pairs = [(i, (i + by) % SECTIONS) for i in range(SECTIONS)]
    return lax.ppermute(array, "section", pairs)


def local(
    layer_input, query_act, key_act, value_act, output_grad, value_weight, norm_gain, top_grad
):
    weight = lax.all_gather(value_weight[0], "seq", axis=0, tiled=True)
    packed = exchange(pack(query_act[0], output_grad[0], key_act[0], value_act[0]))
    packed = packed.reshape(SEQ, 2 * PACK)
    low, high, inverse, dv = attend_probs(packed)
    dv_parts = exchange(dv.reshape(DEVICES, LOCAL, HEAD_DIM))
    grads = attend_grads(packed, low, high, inverse)
    dv_parts, grads = lax.optimization_barrier((dv_parts, grads))
    here = lax.axis_index("section").astype(jnp.int32).reshape(1)
    terms = norm_term(
        here,
        dv_parts,
        weight,
        layer_input[0].reshape(ROWS, D),
        norm_gain,
        top_grad.reshape(ROWS, D),
    )
    grads_back = exchange(grads.reshape(DEVICES, LOCAL, PACK))
    arrived = [
        [terms[half * SECTIONS]] + [turn(terms[half * SECTIONS + k], k) for k in (1, 2, 3)]
        for half in range(HALVES)
    ]
    back = []
    for half in range(HALVES):
        sums = suffix_sums(here, arrived[half])
        back += [sums[0]] + [turn(sums[k], -k) for k in (1, 2, 3)]
    current = place(here, back)
    query_grad, key_grad = unpack(grads_back)
    return current.reshape(1, BATCH, LOCAL, D), query_grad[None], key_grad[None]


def solution(mesh):
    return jax.shard_map(
        local,
        mesh=mesh,
        in_specs=(
            P("section", None, "seq", None),
            P("section", None, "seq", None),
            P("section", None, "seq", None),
            P("section", None, "seq", None),
            P("section", None, "seq", None),
            P("section", "seq", None),
            P("section", None),
            P(None, "seq", None),
        ),
        out_specs=(
            P("section", None, "seq", None),
            P("section", None, "seq", None),
            P("section", None, "seq", None),
        ),
        check_vma=False,
    )
```

profile of v0, /device:TPU:10, one launch (start us, length us, event | category | flops | bytes accessed | tf_op | source)
XLA Modules:
  0.0 239.0 jit_solution(11771477570704993286)
XLA Ops:
  7.9 5.1 %pack.1 = bf16[32,64,1280]{2,1,0:T(8,128)(2,1)} custom-call(bf16[2,64,8192]{2,1,0:T(8,128)(2,1)} %bitcast.24, bf16[2,64,8192]{2,1,0:T(8,128)(2,1)} %bitcast.25, bf16[2,64,1024]{2,1,0:T(8,128)(2,1)} %bitcast.28, bf16[2,64,1024]{2,1,0:T(8,128)(2,1)} %bitcast.29), custom_call_target="tpu_custom_call" | custom-call | flops 6000000000 | tf_op jit(solution)/shard_map/pack/pallas_call | solution.py:58
  13.0 78.0 %all_to_all.15 = bf16[32,64,1280]{2,1,0:T(8,128)(2,1)} all-to-all(bf16[32,64,1280]{2,1,0:T(8,128)(2,1)} %pack.1), channel_id=1, replica_groups=mesh['section'=4,'seq'=32] {'seq'}, dimensions={0} | all-to-all | bytes 10485760 | tf_op jit(solution)/shard_map/all_to_all | solution.py:430
  91.1 28.6 %probs.1 = (bf16[8,4,256,512]{3,2,1,0:T(8,128)(2,1)}, bf16[8,8,256,512]{3,2,1,0:T(8,128)(2,1)}, f32[16,1,512]{2,1,0:T(1,128)}, bf16[2048,128]{1,0:T(8,128)(2,1)}) custom-call(bf16[2048,1280]{1,0:T(8,128)(2,1)} %bitcast.14, bf16[2048,1280]{1,0:T(8,128)(2,1)} %bitcast.15, bf16[2048,1280]{1,0:T(8,128)(2,1)} %bitcast.16), custom_call_target="tpu_custom_call" | custom-call | flops 27000000512 | tf_op jit(solution)/shard_map/probs/pallas_call | solution.py:187
  119.7 5.4 %all-to-all-start.1 = ((bf16[32,64,128]{2,1,0:T(8,128)(2,1)}), bf16[32,64,128]{2,1,0:T(8,128)(2,1)S(1)}, u32[]{:S(2)}, u32[]{:S(2)}) async-start(bf16[32,64,128]{2,1,0:T(8,128)(2,1)} %bitcast.22), calls=%async_computation.1 | async-start | bytes 1048576 | tf_op jit(solution)/shard_map/all_to_all | solution.py:430
  125.1 27.3 %grads.1 = bf16[2048,640]{1,0:T(8,128)(2,1)} custom-call(bf16[2048,1280]{1,0:T(8,128)(2,1)} %bitcast.17, bf16[2048,1280]{1,0:T(8,128)(2,1)} %bitcast.18, bf16[2048,1280]{1,0:T(8,128)(2,1)} %bitcast.19, bf16[2048,1280]{1,0:T(8,128)(2,1)} %bitcast.20, bf16[8,4,256,512]{3,2,1,0:T(8,128)(2,1)} %get-tuple-element.28.low_ref, ...), custom_call_target="tpu_custom_call" | custom-call | flops 27000000512 | tf_op jit(solution)/shard_map/grads/pallas_call | solution.py:266
  153.1 7.5 %all-to-all-start.2 = ((bf16[32,64,640]{2,1,0:T(8,128)(2,1)}), bf16[32,64,640]{2,1,0:T(8,128)(2,1)S(1)}, u32[]{:S(2)}, u32[]{:S(2)}) async-start(bf16[32,64,640]{2,1,0:T(8,128)(2,1)} %bitcast.21), calls=%async_computation.2 | async-start | bytes 5242880 | tf_op jit(solution)/shard_map/all_to_all | solution.py:430
  160.7 17.9 %term.1 = (bf16[16,8192]{1,0:T(8,128)(2,1)}, bf16[16,8192]{1,0:T(8,128)(2,1)}, bf16[16,8192]{1,0:T(8,128)(2,1)}, bf16[16,8192]{1,0:T(8,128)(2,1)}, bf16[16,8192]...) custom-call(s32[1]{0:T(128)} %bitcast.here_ref, ...), custom_call_target="tpu_custom_call" | custom-call | flops 12000000000 | tf_op jit(solution)/shard_map/term/pallas_call | solution.py:352
  178.6 1.6 collective-permute-start.6
  180.1 0.9 collective-permute-start.7
  181.1 2.4 collective-permute-start.8
  183.4 3.4 %collective-permute-start.1 = (bf16[16,8192]{1,0:T(8,128)(2,1)}, bf16[16,8192]{1,0:T(8,128)(2,1)S(1)}, u32[]{:S(2)}, u32[]{:S(2)}) collective-permute-start(bf16[16,8192]{1,0:T(8,128)(2,1)} %get-tuple-element.34), channel_id=1, source_target_pairs={{0,64},{32,96},{64,0},{96,32},{1,65},{33,97},{65,1},{97,33},{2,66}... | collective-permute-start | bytes 786440 | tf_op jit(solution)/shard_map/ppermute | solution.py:435
  186.9 5.4 %collective-permute-done.6.refs_1_ = bf16[16,8192]{1,0:T(8,128)(2,1)S(1)} collective-permute-done((bf16[16,8192]{1,0:T(8,128)(2,1)}, bf16[16,8192]{1,0:T(8,128)(2,1)S(1)}, u32[]{:S(2)}, u32[]{:S(2)}) %collective-permute-start.6) | collective-permute-done | bytes 262176 | tf_op jit(solution)/shard_map/ppermute | solution.py:435
  192.3 4.4 %collective-permute-done.8.refs_3_ = bf16[16,8192]{1,0:T(8,128)(2,1)S(1)} collective-permute-done((bf16[16,8192]{1,0:T(8,128)(2,1)}, bf16[16,8192]{1,0:T(8,128)(2,1)S(1)}, u32[]{:S(2)}, u32[]{:S(2)}) %collective-permute-start.8) | collective-permute-done | bytes 262176 | tf_op jit(solution)/shard_map/ppermute | solution.py:435
  197.4 2.3 suffix_sums.3
  199.8 0.9 collective-permute-start.10
  201.0 1.7 collective-permute-start.9
  202.8 8.9 %collective-permute-done.2.refs_3_ = bf16[16,8192]{1,0:T(8,128)(2,1)} collective-permute-done((bf16[16,8192]{1,0:T(8,128)(2,1)}, bf16[16,8192]{1,0:T(8,128)(2,1)}, u32[]{:S(2)}, u32[]{:S(2)}) %collective-permute-start.2) | collective-permute-done | bytes 262176 | tf_op jit(solution)/shard_map/ppermute | solution.py:435
  211.7 2.3 suffix_sums.2
  214.1 2.0 collective-permute-start.5
  216.1 1.5 copy-done
  217.6 3.9 %unpack.1 = (bf16[2,64,8192]{2,1,0:T(8,128)(2,1)}, bf16[2,64,1024]{2,1,0:T(8,128)(2,1)}) custom-call(bf16[32,64,640]{2,1,0:T(8,128)(2,1)} %copy-done), custom_call_target="tpu_custom_call" | custom-call | flops 5000000000 | tf_op jit(solution)/shard_map/unpack/pallas_call | solution.py:82
  221.6 1.6 collective-permute-done.3.refs_1_
  223.2 6.3 %collective-permute-done.4.refs_2_ = bf16[16,8192]{1,0:T(8,128)(2,1)} collective-permute-done((bf16[16,8192]{1,0:T(8,128)(2,1)}, bf16[16,8192]{1,0:T(8,128)(2,1)}, u32[]{:S(2)}, u32[]{:S(2)}) %collective-permute-start.4) | collective-permute-done | bytes 262176 | tf_op jit(solution)/shard_map/ppermute | solution.py:435
  229.5 2.7 %place.1 = bf16[128,8192]{1,0:T(8,128)(2,1)} custom-call(s32[1]{0:T(128)} %bitcast.here_ref, bf16[16,8192]{1,0:T(8,128)(2,1)} %get-tuple-element.36.refs_0_, bf16[16,8192]{1,0:T(8,128)(2,1)} %collective-permute-done.3.refs_1_, bf16[16,8192]{1,0:T(8,128)(2,1)} %collective-permute-done.4.refs_2_, bf16[16,8192]{1,0:T(8,128)(2,1)} %collective-permute-done.5.refs_3_, ...), custom_call_target="tpu_custom_call" | custom-call | flops 2000000000 | tf_op jit(solution)/shard_map/place/pallas_call | solution.py:417
  (36 shorter events, 2.7 us)
Async XLA Ops:
  7.2 153.5 %all-gather.3.cloned.1.call-start = ((), (), s32[]{:S(2)}) async-start(), calls=%async_computation.3 | async-start | bytes 17301504 | tf_op jit(solution)/shard_map/all_gather | solution.py:441
  119.7 32.7 %all-to-all-start.1 = ((bf16[32,64,128]{2,1,0:T(8,128)(2,1)}), bf16[32,64,128]{2,1,0:T(8,128)(2,1)S(1)}, u32[]{:S(2)}, u32[]{:S(2)}) async-start(bf16[32,64,128]{2,1,0:T(8,128)(2,1)} %bitcast.22), calls=%async_computation.1 | async-start | bytes 1048576 | tf_op jit(solution)/shard_map/all_to_all | solution.py:430
  152.3 0.8 copy-start.1
  153.1 63.0 %all-to-all-start.2 = ((bf16[32,64,640]{2,1,0:T(8,128)(2,1)}), bf16[32,64,640]{2,1,0:T(8,128)(2,1)S(1)}, u32[]{:S(2)}, u32[]{:S(2)}) async-start(bf16[32,64,640]{2,1,0:T(8,128)(2,1)} %bitcast.21), calls=%async_computation.2 | async-start | bytes 5242880 | tf_op jit(solution)/shard_map/all_to_all | solution.py:430
  178.6 13.7 %collective-permute-start.6 = (bf16[16,8192]{1,0:T(8,128)(2,1)}, bf16[16,8192]{1,0:T(8,128)(2,1)S(1)}, u32[]{:S(2)}, u32[]{:S(2)}) collective-permute-start(bf16[16,8192]{1,0:T(8,128)(2,1)} %get-tuple-element.41), channel_id=1, source_target_pairs={{0,32},{32,64},{64,96},{96,0},{1,33},{33,65},{65,97},{97,1},{2,34}... | collective-permute-start | bytes 786440 | tf_op jit(solution)/shard_map/ppermute | solution.py:435
  180.1 12.2 %collective-permute-start.7 = (bf16[16,8192]{1,0:T(8,128)(2,1)}, bf16[16,8192]{1,0:T(8,128)(2,1)S(1)}, u32[]{:S(2)}, u32[]{:S(2)}) collective-permute-start(bf16[16,8192]{1,0:T(8,128)(2,1)} %get-tuple-element.42), channel_id=1, source_target_pairs={{0,64},{32,96},{64,0},{96,32},{1,65},{33,97},{65,1},{97,33},{2,66}... | collective-permute-start | bytes 786440 | tf_op jit(solution)/shard_map/ppermute | solution.py:435
  181.1 15.7 %collective-permute-start.8 = (bf16[16,8192]{1,0:T(8,128)(2,1)}, bf16[16,8192]{1,0:T(8,128)(2,1)S(1)}, u32[]{:S(2)}, u32[]{:S(2)}) collective-permute-start(bf16[16,8192]{1,0:T(8,128)(2,1)} %get-tuple-element.43), channel_id=1, source_target_pairs={{0,96},{32,0},{64,32},{96,64},{1,97},{33,1},{65,33},{97,65},{2,98}... | collective-permute-start | bytes 786440 | tf_op jit(solution)/shard_map/ppermute | solution.py:435
  183.4 17.6 %collective-permute-start = (bf16[16,8192]{1,0:T(8,128)(2,1)}, bf16[16,8192]{1,0:T(8,128)(2,1)S(1)}, u32[]{:S(2)}, u32[]{:S(2)}) collective-permute-start(bf16[16,8192]{1,0:T(8,128)(2,1)} %get-tuple-element.33), channel_id=1, source_target_pairs={{0,32},{32,64},{64,96},{96,0},{1,33},{33,65},{65,97},{97,1},{2,34}... | collective-permute-start | bytes 786440 | tf_op jit(solution)/shard_map/ppermute | solution.py:435
  183.4 19.3 %collective-permute-start.1 = (bf16[16,8192]{1,0:T(8,128)(2,1)}, bf16[16,8192]{1,0:T(8,128)(2,1)S(1)}, u32[]{:S(2)}, u32[]{:S(2)}) collective-permute-start(bf16[16,8192]{1,0:T(8,128)(2,1)} %get-tuple-element.34), channel_id=1, source_target_pairs={{0,64},{32,96},{64,0},{96,32},{1,65},{33,97},{65,1},{97,33},{2,66}... | collective-permute-start | bytes 786440 | tf_op jit(solution)/shard_map/ppermute | solution.py:435
  192.3 4.5 %copy-start.7 = (bf16[16,8192]{1,0:T(8,128)(2,1)}, bf16[16,8192]{1,0:T(8,128)(2,1)S(1)}, u32[]{:S(2)}) copy-start(bf16[16,8192]{1,0:T(8,128)(2,1)S(1)} %collective-permute-done.6.refs_1_) | copy-start | bytes 786436
  192.3 19.4 %collective-permute-start.2 = (bf16[16,8192]{1,0:T(8,128)(2,1)}, bf16[16,8192]{1,0:T(8,128)(2,1)}, u32[]{:S(2)}, u32[]{:S(2)}) collective-permute-start(bf16[16,8192]{1,0:T(8,128)(2,1)} %get-tuple-element.35), channel_id=1, source_target_pairs={{0,96},{32,0},{64,32},{96,64},{1,97},{33,1},{65,33},{97,65},{2,98}... | collective-permute-start | bytes 786440 | tf_op jit(solution)/shard_map/ppermute | solution.py:435
  192.3 4.5 %copy-start.8 = (bf16[16,8192]{1,0:T(8,128)(2,1)}, bf16[16,8192]{1,0:T(8,128)(2,1)S(1)}, u32[]{:S(2)}) copy-start(bf16[16,8192]{1,0:T(8,128)(2,1)S(1)} %collective-permute-done.7.refs_2_) | copy-start | bytes 786436
  199.8 14.4 %collective-permute-start.10 = (bf16[16,8192]{1,0:T(8,128)(2,1)}, bf16[16,8192]{1,0:T(8,128)(2,1)S(1)}, u32[]{:S(2)}, u32[]{:S(2)}) collective-permute-start(bf16[16,8192]{1,0:T(8,128)(2,1)} %get-tuple-element.46), channel_id=1, source_target_pairs={{0,64},{32,96},{64,0},{96,32},{1,65},{33,97},{65,1},{97,33},{2,66}... | collective-permute-start | bytes 786440 | tf_op jit(solution)/shard_map/ppermute | solution.py:435
  200.7 20.8 %collective-permute-start.11 = (bf16[16,8192]{1,0:T(8,128)(2,1)}, bf16[16,8192]{1,0:T(8,128)(2,1)S(1)}, u32[]{:S(2)}, u32[]{:S(2)}) collective-permute-start(bf16[16,8192]{1,0:T(8,128)(2,1)} %get-tuple-element.47), channel_id=1, source_target_pairs={{0,32},{32,64},{64,96},{96,0},{1,33},{33,65},{65,97},{97,1},{2,34}... | collective-permute-start | bytes 786440 | tf_op jit(solution)/shard_map/ppermute | solution.py:435
  201.0 10.6 %copy-start.5 = (bf16[16,8192]{1,0:T(8,128)(2,1)}, bf16[16,8192]{1,0:T(8,128)(2,1)S(1)}, u32[]{:S(2)}) copy-start(bf16[16,8192]{1,0:T(8,128)(2,1)S(1)} %collective-permute-done.refs_1_) | copy-start | bytes 786436
  201.0 20.5 %collective-permute-start.9 = (bf16[16,8192]{1,0:T(8,128)(2,1)}, bf16[16,8192]{1,0:T(8,128)(2,1)S(1)}, u32[]{:S(2)}, u32[]{:S(2)}) collective-permute-start(bf16[16,8192]{1,0:T(8,128)(2,1)} %get-tuple-element.45), channel_id=1, source_target_pairs={{0,96},{32,0},{64,32},{96,64},{1,97},{33,1},{65,33},{97,65},{2,98}... | collective-permute-start | bytes 786440 | tf_op jit(solution)/shard_map/ppermute | solution.py:435
  202.8 8.9 %copy-start.6 = (bf16[16,8192]{1,0:T(8,128)(2,1)}, bf16[16,8192]{1,0:T(8,128)(2,1)S(1)}, u32[]{:S(2)}) copy-start(bf16[16,8192]{1,0:T(8,128)(2,1)S(1)} %collective-permute-done.1.refs_2_) | copy-start | bytes 786436
  214.0 9.2 %collective-permute-start.3 = (bf16[16,8192]{1,0:T(8,128)(2,1)}, bf16[16,8192]{1,0:T(8,128)(2,1)}, u32[]{:S(2)}, u32[]{:S(2)}) collective-permute-start(bf16[16,8192]{1,0:T(8,128)(2,1)} %get-tuple-element.37), channel_id=1, source_target_pairs={{0,96},{32,0},{64,32},{96,64},{1,97},{33,1},{65,33},{97,65},{2,98}... | collective-permute-start | bytes 786440 | tf_op jit(solution)/shard_map/ppermute | solution.py:435
  214.0 15.4 %collective-permute-start.4 = (bf16[16,8192]{1,0:T(8,128)(2,1)}, bf16[16,8192]{1,0:T(8,128)(2,1)}, u32[]{:S(2)}, u32[]{:S(2)}) collective-permute-start(bf16[16,8192]{1,0:T(8,128)(2,1)} %get-tuple-element.38), channel_id=1, source_target_pairs={{0,64},{32,96},{64,0},{96,32},{1,65},{33,97},{65,1},{97,33},{2,66}... | collective-permute-start | bytes 786440 | tf_op jit(solution)/shard_map/ppermute | solution.py:435
  214.1 7.4 %copy-start.2 = (bf16[16,8192]{1,0:T(8,128)(2,1)}, bf16[16,8192]{1,0:T(8,128)(2,1)S(1)}, u32[]{:S(2)}) copy-start(bf16[16,8192]{1,0:T(8,128)(2,1)S(1)} %collective-permute-done.10.refs_6_) | copy-start | bytes 786436
  214.1 15.3 %collective-permute-start.5 = (bf16[16,8192]{1,0:T(8,128)(2,1)}, bf16[16,8192]{1,0:T(8,128)(2,1)}, u32[]{:S(2)}, u32[]{:S(2)}) collective-permute-start(bf16[16,8192]{1,0:T(8,128)(2,1)} %get-tuple-element.39), channel_id=1, source_target_pairs={{0,32},{32,64},{64,96},{96,0},{1,33},{33,65},{65,97},{97,1},{2,34}... | collective-permute-start | bytes 786440 | tf_op jit(solution)/shard_map/ppermute | solution.py:435
  216.1 1.5 copy-start
  221.6 7.9 %copy-start.3 = (bf16[16,8192]{1,0:T(8,128)(2,1)}, bf16[16,8192]{1,0:T(8,128)(2,1)S(1)}, u32[]{:S(2)}) copy-start(bf16[16,8192]{1,0:T(8,128)(2,1)S(1)} %collective-permute-done.11.refs_7_) | copy-start | bytes 786436
  221.6 7.9 %copy-start.4 = (bf16[16,8192]{1,0:T(8,128)(2,1)}, bf16[16,8192]{1,0:T(8,128)(2,1)S(1)}, u32[]{:S(2)}) copy-start(bf16[16,8192]{1,0:T(8,128)(2,1)S(1)} %collective-permute-done.9.refs_5_) | copy-start | bytes 786436
  (1 other events, 0.7 us)
Sparse Core Ops, SparseCore 0:
  10.3 131.5 all-gather.2
where the time goes:
time: 240 us; the launch traced here: 239 us
  Pallas kernels  90.1 us (38%)
  blocking collectives  78 us (32%)
  waiting for transfers between devices  27.4 us (11%)
  starting transfers between devices  26.3 us (11%)
  between operations  14.1 us (6%)
  local copies, waits for them, and re-layouts  3.03 us (1%)
    all_to_all x1, blocking collectives, exchange(): return lax.all_to_all(parts, 'seq', 0, 0, tiled=True)  78 us
    pallas_call x1, Pallas kernels, attend_probs(): pl.pallas_call(probs_body, grid=(STEPS,), out_shape=(jax.ShapeDtypeStruct...  28.6 us
    pallas_call x1, Pallas kernels, attend_grads(): pl.pallas_call(grads_body, grid=(STEPS,), out_shape=jax.ShapeDtypeStruct(...  27.3 us
    ppermute x12, waiting for transfers between devices, turn(): return lax.ppermute(array, 'section', pairs)  26.7 us
    pallas_call x1, Pallas kernels, norm_term(): pl.pallas_call(term_body, grid=(D // width,), out_shape=(jax.ShapeDtypeSt...  17.9 us
    ppermute x12, starting transfers between devices, turn(): return lax.ppermute(array, 'section', pairs)  13.4 us
    all_to_all x2, starting transfers between devices, exchange(): return lax.all_to_all(parts, 'seq', 0, 0, tiled=True)  12.9 us
    pallas_call x1, Pallas kernels, pack(): pl.pallas_call(pack_body, grid=(BATCH, per_seq), out_shape=jax.ShapeDtype...  5.15 us
  transfers between devices with their start and end apart: 15, of which 5 were waited for; matrix products, arithmetic and copies ran while one was open for 0% of the time, Pallas kernels for 37%

commit v1 on v0

--- a/solution.py
+++ b/solution.py
@@ -297,6 +297,10 @@
             emit(seq, slice(head * HEAD_DIM, (head + 1) * HEAD_DIM), total.astype(BF))
 
 
+def halves_sum(piece):
+    return piece[:, :HEAD_DIM] + piece[:, HEAD_DIM:]
+
+
 def term_body(here_ref, parts_ref, w_ref, x_ref, gain_ref, top_ref, *refs):
     out_refs, (vg_ref, u_ref, xs_ref, acc) = refs[:-4], refs[-4:]
     step = pl.program_id(0)
@@ -312,30 +316,31 @@
         pair_sums(parts_ref, emit)
 
     dots = lax.dot_general(vg_ref[...], w_ref[...], LAST, preferred_element_type=F32)
-    squares = jnp.zeros((ROWS, 1), F32)
-    inner = jnp.zeros((ROWS, 1), F32)
+    squares = acc[0]
+    inner = acc[1]
     for i in range(PIECES):
         cols = slice(i * FEATS, (i + 1) * FEATS)
         x = x_ref[:, cols].astype(F32)
         u = dots[:, cols] * gain_ref[:, cols]
         u_ref[step * PIECES + i] = u
         xs_ref[step * PIECES + i] = x_ref[:, cols]
-        squares = squares + jnp.sum(x * x, axis=1, keepdims=True)
-        inner = inner + jnp.sum(x * u, axis=1, keepdims=True)
-    acc[0] += squares
-    acc[1] += inner
+        squares = squares + halves_sum(x * x)
+        inner = inner + halves_sum(x * u)
+    acc[0] = squares
+    acc[1] = inner
 
     @pl.when(step == pl.num_programs(0) - 1)
     def _():
         flag = jnp.where(here == SECTIONS - 1, 1.0, 0.0).astype(F32)
-        r = lax.rsqrt(acc[0] * (1.0 / D) + 1e-05)
-        acc[1] = acc[1] * (1.0 / D) * (r * r * r)
-        acc[0] = r
+        r = lax.rsqrt(jnp.sum(acc[0], axis=1, keepdims=True) * (1.0 / D) + 1e-05)
+        inner = jnp.sum(acc[1], axis=1, keepdims=True) * (1.0 / D) * (r * r * r)
+        acc[0] = jnp.broadcast_to(r, (ROWS, HEAD_DIM))
+        acc[1] = jnp.broadcast_to(inner, (ROWS, HEAD_DIM))
         for half in range(HALVES * SECTIONS):
             first = ((here + half % SECTIONS) % SECTIONS * HALVES + half // SECTIONS) * PART
             rows = pl.ds(pl.multiple_of(first, PART), PART)
-            r = acc[0, rows, :]
-            inner = acc[1, rows, :]
+            r = jnp.concatenate([acc[0, rows, :]] * (FEATS // HEAD_DIM), axis=1)
+            inner = jnp.concatenate([acc[1, rows, :]] * (FEATS // HEAD_DIM), axis=1)
 
             def finish(i, carry):
                 cols = pl.ds(pl.multiple_of(i * FEATS, FEATS), FEATS)
@@ -344,7 +349,7 @@
                 out_refs[half][:, cols] = term.astype(BF)
                 return carry
 
-            lax.fori_loop(0, D // FEATS, finish, 0, unroll=4)
+            lax.fori_loop(0, D // FEATS, finish, 0, unroll=16)
 
 
 def norm_term(here, parts, weight, x, gain, top):
@@ -366,7 +371,7 @@
             pltpu.VMEM((ROWS, KV_HEADS * HEAD_DIM), BF),
             pltpu.VMEM((D // FEATS, ROWS, FEATS), F32),
             pltpu.VMEM((D // FEATS, ROWS, FEATS), BF),
-            pltpu.VMEM((2, ROWS, 1), F32),
+            pltpu.VMEM((2, ROWS, HEAD_DIM), F32),
         ],
         compiler_params=PARAMS,
         cost_estimate=cost(12),

time: 240 us -> 235 us (0.979)
  Pallas kernels: 90.1 us -> 85.5 us
    pallas_call x1, Pallas kernels: 17.9 us -> 13.3 us  [norm_term(): pl.pallas_call(term_body, grid=(D // width,), out_shape=(jax.ShapeDtypeSt...]
  transfers between devices with their start and end apart: 15 -> 15, of which waited for: 5 -> 5; matrix products, arithmetic and copies ran while one was open for 0% -> 0% of each run, Pallas kernels for 37% -> 35%
where the time goes in v1:
time: 235 us; the launch traced here: 234 us
  Pallas kernels  85.5 us (36%)
  blocking collectives  78 us (33%)
  waiting for transfers between devices  27.4 us (12%)
  starting transfers between devices  26.3 us (11%)
  between operations  14.1 us (6%)
  local copies, waits for them, and re-layouts  3.03 us (1%)
    all_to_all x1, blocking collectives, exchange(): return lax.all_to_all(parts, 'seq', 0, 0, tiled=True)  78 us
    pallas_call x1, Pallas kernels, attend_probs(): pl.pallas_call(probs_body, grid=(STEPS,), out_shape=(jax.ShapeDtypeStruct...  28.6 us
    pallas_call x1, Pallas kernels, attend_grads(): pl.pallas_call(grads_body, grid=(STEPS,), out_shape=jax.ShapeDtypeStruct(...  27.3 us
    ppermute x12, waiting for transfers between devices, turn(): return lax.ppermute(array, 'section', pairs)  26.7 us
    ppermute x12, starting transfers between devices, turn(): return lax.ppermute(array, 'section', pairs)  13.4 us
    pallas_call x1, Pallas kernels, norm_term(): pl.pallas_call(term_body, grid=(D // width,), out_shape=(jax.ShapeDtypeSt...  13.3 us
    all_to_all x2, starting transfers between devices, exchange(): return lax.all_to_all(parts, 'seq', 0, 0, tiled=True)  12.9 us
    pallas_call x1, Pallas kernels, pack(): pl.pallas_call(pack_body, grid=(BATCH, per_seq), out_shape=jax.ShapeDtype...  5.15 us
  transfers between devices with their start and end apart: 15, of which 5 were waited for; matrix products, arithmetic and copies ran while one was open for 0% of the time, Pallas kernels for 35%

profile of v1, /device:TPU:10, one launch (start us, length us, event | category | flops | bytes accessed | tf_op | source)
XLA Modules:
  0.0 234.4 jit_solution(6915277677355196746)
XLA Ops:
  7.9 5.1 %pack.1 = bf16[32,64,1280]{2,1,0:T(8,128)(2,1)} custom-call(bf16[2,64,8192]{2,1,0:T(8,128)(2,1)} %bitcast.24, bf16[2,64,8192]{2,1,0:T(8,128)(2,1)} %bitcast.25, bf16[2,64,1024]{2,1,0:T(8,128)(2,1)} %bitcast.28, bf16[2,64,1024]{2,1,0:T(8,128)(2,1)} %bitcast.29), custom_call_target="tpu_custom_call" | custom-call | flops 6000000000 | tf_op jit(solution)/shard_map/pack/pallas_call | solution.py:58
  13.0 78.0 %all_to_all.15 = bf16[32,64,1280]{2,1,0:T(8,128)(2,1)} all-to-all(bf16[32,64,1280]{2,1,0:T(8,128)(2,1)} %pack.1), channel_id=1, replica_groups=mesh['section'=4,'seq'=32] {'seq'}, dimensions={0} | all-to-all | bytes 10485760 | tf_op jit(solution)/shard_map/all_to_all | solution.py:435
  91.1 28.6 %probs.1 = (bf16[8,4,256,512]{3,2,1,0:T(8,128)(2,1)}, bf16[8,8,256,512]{3,2,1,0:T(8,128)(2,1)}, f32[16,1,512]{2,1,0:T(1,128)}, bf16[2048,128]{1,0:T(8,128)(2,1)}) custom-call(bf16[2048,1280]{1,0:T(8,128)(2,1)} %bitcast.14, bf16[2048,1280]{1,0:T(8,128)(2,1)} %bitcast.15, bf16[2048,1280]{1,0:T(8,128)(2,1)} %bitcast.16), custom_call_target="tpu_custom_call" | custom-call | flops 27000000512 | tf_op jit(solution)/shard_map/probs/pallas_call | solution.py:187
  119.7 5.4 %all-to-all-start.1 = ((bf16[32,64,128]{2,1,0:T(8,128)(2,1)}), bf16[32,64,128]{2,1,0:T(8,128)(2,1)S(1)}, u32[]{:S(2)}, u32[]{:S(2)}) async-start(bf16[32,64,128]{2,1,0:T(8,128)(2,1)} %bitcast.22), calls=%async_computation.1 | async-start | bytes 1048576 | tf_op jit(solution)/shard_map/all_to_all | solution.py:435
  125.1 27.3 %grads.1 = bf16[2048,640]{1,0:T(8,128)(2,1)} custom-call(bf16[2048,1280]{1,0:T(8,128)(2,1)} %bitcast.17, bf16[2048,1280]{1,0:T(8,128)(2,1)} %bitcast.18, bf16[2048,1280]{1,0:T(8,128)(2,1)} %bitcast.19, bf16[2048,1280]{1,0:T(8,128)(2,1)} %bitcast.20, bf16[8,4,256,512]{3,2,1,0:T(8,128)(2,1)} %get-tuple-element.28.low_ref, ...), custom_call_target="tpu_custom_call" | custom-call | flops 27000000512 | tf_op jit(solution)/shard_map/grads/pallas_call | solution.py:266
  153.1 7.5 %all-to-all-start.2 = ((bf16[32,64,640]{2,1,0:T(8,128)(2,1)}), bf16[32,64,640]{2,1,0:T(8,128)(2,1)S(1)}, u32[]{:S(2)}, u32[]{:S(2)}) async-start(bf16[32,64,640]{2,1,0:T(8,128)(2,1)} %bitcast.21), calls=%async_computation.2 | async-start | bytes 5242880 | tf_op jit(solution)/shard_map/all_to_all | solution.py:435
  160.7 13.3 %term.1 = (bf16[16,8192]{1,0:T(8,128)(2,1)}, bf16[16,8192]{1,0:T(8,128)(2,1)}, bf16[16,8192]{1,0:T(8,128)(2,1)}, bf16[16,8192]{1,0:T(8,128)(2,1)}, bf16[16,8192]...) custom-call(s32[1]{0:T(128)} %bitcast.here_ref, ...), custom_call_target="tpu_custom_call" | custom-call | flops 12000000000 | tf_op jit(solution)/shard_map/term/pallas_call | solution.py:357
  173.9 1.6 collective-permute-start.6
  175.5 0.9 collective-permute-start.7
  176.5 2.4 %collective-permute-start.8 = (bf16[16,8192]{1,0:T(8,128)(2,1)}, bf16[16,8192]{1,0:T(8,128)(2,1)S(1)}, u32[]{:S(2)}, u32[]{:S(2)}) collective-permute-start(bf16[16,8192]{1,0:T(8,128)(2,1)} %get-tuple-element.43), channel_id=1, source_target_pairs={{0,96},{32,0},{64,32},{96,64},{1,97},{33,1},{65,33},{97,65},{2,98}... | collective-permute-start | bytes 786440 | tf_op jit(solution)/shard_map/ppermute | solution.py:440
  178.8 3.4 %collective-permute-start.1 = (bf16[16,8192]{1,0:T(8,128)(2,1)}, bf16[16,8192]{1,0:T(8,128)(2,1)S(1)}, u32[]{:S(2)}, u32[]{:S(2)}) collective-permute-start(bf16[16,8192]{1,0:T(8,128)(2,1)} %get-tuple-element.34), channel_id=1, source_target_pairs={{0,64},{32,96},{64,0},{96,32},{1,65},{33,97},{65,1},{97,33},{2,66}... | collective-permute-start | bytes 786440 | tf_op jit(solution)/shard_map/ppermute | solution.py:440
  182.3 5.4 %collective-permute-done.6.refs_1_ = bf16[16,8192]{1,0:T(8,128)(2,1)S(1)} collective-permute-done((bf16[16,8192]{1,0:T(8,128)(2,1)}, bf16[16,8192]{1,0:T(8,128)(2,1)S(1)}, u32[]{:S(2)}, u32[]{:S(2)}) %collective-permute-start.6) | collective-permute-done | bytes 262176 | tf_op jit(solution)/shard_map/ppermute | solution.py:440
  187.7 4.5 %collective-permute-done.8.refs_3_ = bf16[16,8192]{1,0:T(8,128)(2,1)S(1)} collective-permute-done((bf16[16,8192]{1,0:T(8,128)(2,1)}, bf16[16,8192]{1,0:T(8,128)(2,1)S(1)}, u32[]{:S(2)}, u32[]{:S(2)}) %collective-permute-start.8) | collective-permute-done | bytes 262176 | tf_op jit(solution)/shard_map/ppermute | solution.py:440
  192.8 2.3 suffix_sums.3
  195.2 0.9 collective-permute-start.10
  196.4 1.7 collective-permute-start.9
  198.1 8.9 %collective-permute-done.2.refs_3_ = bf16[16,8192]{1,0:T(8,128)(2,1)} collective-permute-done((bf16[16,8192]{1,0:T(8,128)(2,1)}, bf16[16,8192]{1,0:T(8,128)(2,1)}, u32[]{:S(2)}, u32[]{:S(2)}) %collective-permute-start.2) | collective-permute-done | bytes 262176 | tf_op jit(solution)/shard_map/ppermute | solution.py:440
  207.1 2.3 suffix_sums.2
  209.5 2.0 collective-permute-start.5
  211.5 1.5 copy-done
  213.0 3.9 %unpack.1 = (bf16[2,64,8192]{2,1,0:T(8,128)(2,1)}, bf16[2,64,1024]{2,1,0:T(8,128)(2,1)}) custom-call(bf16[32,64,640]{2,1,0:T(8,128)(2,1)} %copy-done), custom_call_target="tpu_custom_call" | custom-call | flops 5000000000 | tf_op jit(solution)/shard_map/unpack/pallas_call | solution.py:82
  217.0 1.6 collective-permute-done.3.refs_1_
  218.6 6.3 %collective-permute-done.4.refs_2_ = bf16[16,8192]{1,0:T(8,128)(2,1)} collective-permute-done((bf16[16,8192]{1,0:T(8,128)(2,1)}, bf16[16,8192]{1,0:T(8,128)(2,1)}, u32[]{:S(2)}, u32[]{:S(2)}) %collective-permute-start.4) | collective-permute-done | bytes 262176 | tf_op jit(solution)/shard_map/ppermute | solution.py:440
  224.9 2.7 %place.1 = bf16[128,8192]{1,0:T(8,128)(2,1)} custom-call(s32[1]{0:T(128)} %bitcast.here_ref, bf16[16,8192]{1,0:T(8,128)(2,1)} %get-tuple-element.36.refs_0_, bf16[16,8192]{1,0:T(8,128)(2,1)} %collective-permute-done.3.refs_1_, bf16[16,8192]{1,0:T(8,128)(2,1)} %collective-permute-done.4.refs_2_, bf16[16,8192]{1,0:T(8,128)(2,1)} %collective-permute-done.5.refs_3_, ...), custom_call_target="tpu_custom_call" | custom-call | flops 2000000000 | tf_op jit(solution)/shard_map/place/pallas_call | solution.py:422
  (36 shorter events, 2.7 us)
Async XLA Ops:
  7.2 153.5 %all-gather.3.cloned.1.call-start = ((), (), s32[]{:S(2)}) async-start(), calls=%async_computation.3 | async-start | bytes 17301504 | tf_op jit(solution)/shard_map/all_gather | solution.py:446
  119.7 32.7 %all-to-all-start.1 = ((bf16[32,64,128]{2,1,0:T(8,128)(2,1)}), bf16[32,64,128]{2,1,0:T(8,128)(2,1)S(1)}, u32[]{:S(2)}, u32[]{:S(2)}) async-start(bf16[32,64,128]{2,1,0:T(8,128)(2,1)} %bitcast.22), calls=%async_computation.1 | async-start | bytes 1048576 | tf_op jit(solution)/shard_map/all_to_all | solution.py:435
  152.3 0.8 copy-start.1
  153.1 58.4 %all-to-all-start.2 = ((bf16[32,64,640]{2,1,0:T(8,128)(2,1)}), bf16[32,64,640]{2,1,0:T(8,128)(2,1)S(1)}, u32[]{:S(2)}, u32[]{:S(2)}) async-start(bf16[32,64,640]{2,1,0:T(8,128)(2,1)} %bitcast.21), calls=%async_computation.2 | async-start | bytes 5242880 | tf_op jit(solution)/shard_map/all_to_all | solution.py:435
  173.9 13.7 %collective-permute-start.6 = (bf16[16,8192]{1,0:T(8,128)(2,1)}, bf16[16,8192]{1,0:T(8,128)(2,1)S(1)}, u32[]{:S(2)}, u32[]{:S(2)}) collective-permute-start(bf16[16,8192]{1,0:T(8,128)(2,1)} %get-tuple-element.41), channel_id=1, source_target_pairs={{0,32},{32,64},{64,96},{96,0},{1,33},{33,65},{65,97},{97,1},{2,34}... | collective-permute-start | bytes 786440 | tf_op jit(solution)/shard_map/ppermute | solution.py:440
  175.5 12.2 %collective-permute-start.7 = (bf16[16,8192]{1,0:T(8,128)(2,1)}, bf16[16,8192]{1,0:T(8,128)(2,1)S(1)}, u32[]{:S(2)}, u32[]{:S(2)}) collective-permute-start(bf16[16,8192]{1,0:T(8,128)(2,1)} %get-tuple-element.42), channel_id=1, source_target_pairs={{0,64},{32,96},{64,0},{96,32},{1,65},{33,97},{65,1},{97,33},{2,66}... | collective-permute-start | bytes 786440 | tf_op jit(solution)/shard_map/ppermute | solution.py:440
  176.5 15.7 %collective-permute-start.8 = (bf16[16,8192]{1,0:T(8,128)(2,1)}, bf16[16,8192]{1,0:T(8,128)(2,1)S(1)}, u32[]{:S(2)}, u32[]{:S(2)}) collective-permute-start(bf16[16,8192]{1,0:T(8,128)(2,1)} %get-tuple-element.43), channel_id=1, source_target_pairs={{0,96},{32,0},{64,32},{96,64},{1,97},{33,1},{65,33},{97,65},{2,98}... | collective-permute-start | bytes 786440 | tf_op jit(solution)/shard_map/ppermute | solution.py:440
  178.8 17.6 %collective-permute-start = (bf16[16,8192]{1,0:T(8,128)(2,1)}, bf16[16,8192]{1,0:T(8,128)(2,1)S(1)}, u32[]{:S(2)}, u32[]{:S(2)}) collective-permute-start(bf16[16,8192]{1,0:T(8,128)(2,1)} %get-tuple-element.33), channel_id=1, source_target_pairs={{0,32},{32,64},{64,96},{96,0},{1,33},{33,65},{65,97},{97,1},{2,34}... | collective-permute-start | bytes 786440 | tf_op jit(solution)/shard_map/ppermute | solution.py:440
  178.8 19.3 %collective-permute-start.1 = (bf16[16,8192]{1,0:T(8,128)(2,1)}, bf16[16,8192]{1,0:T(8,128)(2,1)S(1)}, u32[]{:S(2)}, u32[]{:S(2)}) collective-permute-start(bf16[16,8192]{1,0:T(8,128)(2,1)} %get-tuple-element.34), channel_id=1, source_target_pairs={{0,64},{32,96},{64,0},{96,32},{1,65},{33,97},{65,1},{97,33},{2,66}... | collective-permute-start | bytes 786440 | tf_op jit(solution)/shard_map/ppermute | solution.py:440
  187.7 4.5 %copy-start.7 = (bf16[16,8192]{1,0:T(8,128)(2,1)}, bf16[16,8192]{1,0:T(8,128)(2,1)S(1)}, u32[]{:S(2)}) copy-start(bf16[16,8192]{1,0:T(8,128)(2,1)S(1)} %collective-permute-done.6.refs_1_) | copy-start | bytes 786436
  187.7 19.4 %collective-permute-start.2 = (bf16[16,8192]{1,0:T(8,128)(2,1)}, bf16[16,8192]{1,0:T(8,128)(2,1)}, u32[]{:S(2)}, u32[]{:S(2)}) collective-permute-start(bf16[16,8192]{1,0:T(8,128)(2,1)} %get-tuple-element.35), channel_id=1, source_target_pairs={{0,96},{32,0},{64,32},{96,64},{1,97},{33,1},{65,33},{97,65},{2,98}... | collective-permute-start | bytes 786440 | tf_op jit(solution)/shard_map/ppermute | solution.py:440
  187.7 4.5 %copy-start.8 = (bf16[16,8192]{1,0:T(8,128)(2,1)}, bf16[16,8192]{1,0:T(8,128)(2,1)S(1)}, u32[]{:S(2)}) copy-start(bf16[16,8192]{1,0:T(8,128)(2,1)S(1)} %collective-permute-done.7.refs_2_) | copy-start | bytes 786436
  195.2 14.3 %collective-permute-start.10 = (bf16[16,8192]{1,0:T(8,128)(2,1)}, bf16[16,8192]{1,0:T(8,128)(2,1)S(1)}, u32[]{:S(2)}, u32[]{:S(2)}) collective-permute-start(bf16[16,8192]{1,0:T(8,128)(2,1)} %get-tuple-element.46), channel_id=1, source_target_pairs={{0,64},{32,96},{64,0},{96,32},{1,65},{33,97},{65,1},{97,33},{2,66}... | collective-permute-start | bytes 786440 | tf_op jit(solution)/shard_map/ppermute | solution.py:440
  196.1 20.8 %collective-permute-start.11 = (bf16[16,8192]{1,0:T(8,128)(2,1)}, bf16[16,8192]{1,0:T(8,128)(2,1)S(1)}, u32[]{:S(2)}, u32[]{:S(2)}) collective-permute-start(bf16[16,8192]{1,0:T(8,128)(2,1)} %get-tuple-element.47), channel_id=1, source_target_pairs={{0,32},{32,64},{64,96},{96,0},{1,33},{33,65},{65,97},{97,1},{2,34}... | collective-permute-start | bytes 786440 | tf_op jit(solution)/shard_map/ppermute | solution.py:440
  196.4 10.7 %copy-start.5 = (bf16[16,8192]{1,0:T(8,128)(2,1)}, bf16[16,8192]{1,0:T(8,128)(2,1)S(1)}, u32[]{:S(2)}) copy-start(bf16[16,8192]{1,0:T(8,128)(2,1)S(1)} %collective-permute-done.refs_1_) | copy-start | bytes 786436
  196.4 20.5 %collective-permute-start.9 = (bf16[16,8192]{1,0:T(8,128)(2,1)}, bf16[16,8192]{1,0:T(8,128)(2,1)S(1)}, u32[]{:S(2)}, u32[]{:S(2)}) collective-permute-start(bf16[16,8192]{1,0:T(8,128)(2,1)} %get-tuple-element.45), channel_id=1, source_target_pairs={{0,96},{32,0},{64,32},{96,64},{1,97},{33,1},{65,33},{97,65},{2,98}... | collective-permute-start | bytes 786440 | tf_op jit(solution)/shard_map/ppermute | solution.py:440
  198.1 8.9 %copy-start.6 = (bf16[16,8192]{1,0:T(8,128)(2,1)}, bf16[16,8192]{1,0:T(8,128)(2,1)S(1)}, u32[]{:S(2)}) copy-start(bf16[16,8192]{1,0:T(8,128)(2,1)S(1)} %collective-permute-done.1.refs_2_) | copy-start | bytes 786436
  209.4 9.2 %collective-permute-start.3 = (bf16[16,8192]{1,0:T(8,128)(2,1)}, bf16[16,8192]{1,0:T(8,128)(2,1)}, u32[]{:S(2)}, u32[]{:S(2)}) collective-permute-start(bf16[16,8192]{1,0:T(8,128)(2,1)} %get-tuple-element.37), channel_id=1, source_target_pairs={{0,96},{32,0},{64,32},{96,64},{1,97},{33,1},{65,33},{97,65},{2,98}... | collective-permute-start | bytes 786440 | tf_op jit(solution)/shard_map/ppermute | solution.py:440
  209.4 15.4 %collective-permute-start.4 = (bf16[16,8192]{1,0:T(8,128)(2,1)}, bf16[16,8192]{1,0:T(8,128)(2,1)}, u32[]{:S(2)}, u32[]{:S(2)}) collective-permute-start(bf16[16,8192]{1,0:T(8,128)(2,1)} %get-tuple-element.38), channel_id=1, source_target_pairs={{0,64},{32,96},{64,0},{96,32},{1,65},{33,97},{65,1},{97,33},{2,66}... | collective-permute-start | bytes 786440 | tf_op jit(solution)/shard_map/ppermute | solution.py:440
  209.5 7.4 %copy-start.2 = (bf16[16,8192]{1,0:T(8,128)(2,1)}, bf16[16,8192]{1,0:T(8,128)(2,1)S(1)}, u32[]{:S(2)}) copy-start(bf16[16,8192]{1,0:T(8,128)(2,1)S(1)} %collective-permute-done.10.refs_6_) | copy-start | bytes 786436
  209.5 15.3 %collective-permute-start.5 = (bf16[16,8192]{1,0:T(8,128)(2,1)}, bf16[16,8192]{1,0:T(8,128)(2,1)}, u32[]{:S(2)}, u32[]{:S(2)}) collective-permute-start(bf16[16,8192]{1,0:T(8,128)(2,1)} %get-tuple-element.39), channel_id=1, source_target_pairs={{0,32},{32,64},{64,96},{96,0},{1,33},{33,65},{65,97},{97,1},{2,34}... | collective-permute-start | bytes 786440 | tf_op jit(solution)/shard_map/ppermute | solution.py:440
  211.5 1.5 copy-start
  216.9 7.9 %copy-start.3 = (bf16[16,8192]{1,0:T(8,128)(2,1)}, bf16[16,8192]{1,0:T(8,128)(2,1)S(1)}, u32[]{:S(2)}) copy-start(bf16[16,8192]{1,0:T(8,128)(2,1)S(1)} %collective-permute-done.11.refs_7_) | copy-start | bytes 786436
  217.0 7.9 %copy-start.4 = (bf16[16,8192]{1,0:T(8,128)(2,1)}, bf16[16,8192]{1,0:T(8,128)(2,1)S(1)}, u32[]{:S(2)}) copy-start(bf16[16,8192]{1,0:T(8,128)(2,1)S(1)} %collective-permute-done.9.refs_5_) | copy-start | bytes 786436
  (1 other events, 0.7 us)
Sparse Core Ops, SparseCore 0:
  10.3 131.5 all-gather.2

commit v2 on v1

--- a/solution.py
+++ b/solution.py
@@ -35,6 +35,7 @@
 
 
 PARAMS = pltpu.CompilerParams(vmem_limit_bytes=60 << 20)
+SMALL = pltpu.CompilerParams(vmem_limit_bytes=32 << 20)
 
 
 def cost(us):
@@ -92,7 +93,7 @@
             pl.BlockSpec((None, LOCAL, STEP_UNITS // 2 * HEAD_DIM), lambda b, i: (b, 0, i)),
         ),
         cost_estimate=cost(5),
-        compiler_params=PARAMS,
+        compiler_params=SMALL,
         name="unpack",
     )(parts)
 
@@ -402,7 +403,7 @@
         in_specs=[pl.BlockSpec(memory_space=pltpu.SMEM)] + [spec] * SECTIONS,
         out_specs=(spec,) * SECTIONS,
         cost_estimate=cost(2),
-        compiler_params=PARAMS,
+        compiler_params=SMALL,
         name="suffix_sums",
     )(here, *parts)
 
@@ -426,7 +427,7 @@
         in_specs=[pl.BlockSpec(memory_space=pltpu.SMEM)] + [spec] * (HALVES * SECTIONS),
         out_specs=pl.BlockSpec((ROWS, cols), lambda i: (0, i)),
         cost_estimate=cost(2),
-        compiler_params=PARAMS,
+        compiler_params=SMALL,
         name="place",
     )(here, *parts)
 

time: 235 us -> 235 us (level)
  waiting for transfers between devices: 27.4 us -> 31.6 us
  Pallas kernels: 85.5 us -> 81.5 us
    ppermute x12, waiting for transfers between devices: 26.7 us -> 30.9 us  [turn(): return lax.ppermute(array, 'section', pairs)]
  transfers between devices with their start and end apart: 15 -> 15, of which waited for: 5 -> 6; matrix products, arithmetic and copies ran while one was open for 0% -> 0% of each run, Pallas kernels for 35% -> 34%
where the time goes in v2:
time: 235 us; the launch traced here: 234 us
  Pallas kernels  81.5 us (35%)
  blocking collectives  78 us (33%)
  waiting for transfers between devices  31.6 us (13%)
  starting transfers between devices  26.4 us (11%)
  between operations  14.1 us (6%)
  local copies, waits for them, and re-layouts  2.47 us (1%)
    all_to_all x1, blocking collectives, exchange(): return lax.all_to_all(parts, 'seq', 0, 0, tiled=True)  78 us
    ppermute x12, waiting for transfers between devices, turn(): return lax.ppermute(array, 'section', pairs)  30.9 us
    pallas_call x1, Pallas kernels, attend_probs(): pl.pallas_call(probs_body, grid=(STEPS,), out_shape=(jax.ShapeDtypeStruct...  28.6 us
    pallas_call x1, Pallas kernels, attend_grads(): pl.pallas_call(grads_body, grid=(STEPS,), out_shape=jax.ShapeDtypeStruct(...  27.3 us
    ppermute x12, starting transfers between devices, turn(): return lax.ppermute(array, 'section', pairs)  13.5 us
    pallas_call x1, Pallas kernels, norm_term(): pl.pallas_call(term_body, grid=(D // width,), out_shape=(jax.ShapeDtypeSt...  13.3 us
    all_to_all x2, starting transfers between devices, exchange(): return lax.all_to_all(parts, 'seq', 0, 0, tiled=True)  12.9 us
    pallas_call x1, Pallas kernels, pack(): pl.pallas_call(pack_body, grid=(BATCH, per_seq), out_shape=jax.ShapeDtype...  5.15 us
  transfers between devices with their start and end apart: 15, of which 6 were waited for; matrix products, arithmetic and copies ran while one was open for 0% of the time, Pallas kernels for 34%

profile of v2, /device:TPU:10, one launch (start us, length us, event | category | flops | bytes accessed | tf_op | source)
XLA Modules:
  0.0 234.2 jit_solution(9654300103774156221)
XLA Ops:
  7.9 5.1 %pack.1 = bf16[32,64,1280]{2,1,0:T(8,128)(2,1)} custom-call(bf16[2,64,8192]{2,1,0:T(8,128)(2,1)} %bitcast.24, bf16[2,64,8192]{2,1,0:T(8,128)(2,1)} %bitcast.25, bf16[2,64,1024]{2,1,0:T(8,128)(2,1)} %bitcast.28, bf16[2,64,1024]{2,1,0:T(8,128)(2,1)} %bitcast.29), custom_call_target="tpu_custom_call" | custom-call | flops 6000000000 | tf_op jit(solution)/shard_map/pack/pallas_call | solution.py:59
  13.0 78.0 %all_to_all.15 = bf16[32,64,1280]{2,1,0:T(8,128)(2,1)} all-to-all(bf16[32,64,1280]{2,1,0:T(8,128)(2,1)} %pack.1), channel_id=1, replica_groups=mesh['section'=4,'seq'=32] {'seq'}, dimensions={0} | all-to-all | bytes 10485760 | tf_op jit(solution)/shard_map/all_to_all | solution.py:436
  91.1 28.6 %probs.1 = (bf16[8,4,256,512]{3,2,1,0:T(8,128)(2,1)}, bf16[8,8,256,512]{3,2,1,0:T(8,128)(2,1)}, f32[16,1,512]{2,1,0:T(1,128)}, bf16[2048,128]{1,0:T(8,128)(2,1)}) custom-call(bf16[2048,1280]{1,0:T(8,128)(2,1)} %bitcast.14, bf16[2048,1280]{1,0:T(8,128)(2,1)} %bitcast.15, bf16[2048,1280]{1,0:T(8,128)(2,1)} %bitcast.16), custom_call_target="tpu_custom_call" | custom-call | flops 27000000512 | tf_op jit(solution)/shard_map/probs/pallas_call | solution.py:188
  119.7 5.4 %all-to-all-start.1 = ((bf16[32,64,128]{2,1,0:T(8,128)(2,1)}), bf16[32,64,128]{2,1,0:T(8,128)(2,1)S(1)}, u32[]{:S(2)}, u32[]{:S(2)}) async-start(bf16[32,64,128]{2,1,0:T(8,128)(2,1)} %bitcast.22), calls=%async_computation.1 | async-start | bytes 1048576 | tf_op jit(solution)/shard_map/all_to_all | solution.py:436
  125.1 27.3 %grads.1 = bf16[2048,640]{1,0:T(8,128)(2,1)} custom-call(bf16[2048,1280]{1,0:T(8,128)(2,1)} %bitcast.17, bf16[2048,1280]{1,0:T(8,128)(2,1)} %bitcast.18, bf16[2048,1280]{1,0:T(8,128)(2,1)} %bitcast.19, bf16[2048,1280]{1,0:T(8,128)(2,1)} %bitcast.20, bf16[8,4,256,512]{3,2,1,0:T(8,128)(2,1)} %get-tuple-element.28.low_ref, ...), custom_call_target="tpu_custom_call" | custom-call | flops 27000000512 | tf_op jit(solution)/shard_map/grads/pallas_call | solution.py:267
  153.1 7.5 %all-to-all-start.2 = ((bf16[32,64,640]{2,1,0:T(8,128)(2,1)}), bf16[32,64,640]{2,1,0:T(8,128)(2,1)S(1)}, u32[]{:S(2)}, u32[]{:S(2)}) async-start(bf16[32,64,640]{2,1,0:T(8,128)(2,1)} %bitcast.21), calls=%async_computation.2 | async-start | bytes 5242880 | tf_op jit(solution)/shard_map/all_to_all | solution.py:436
  160.7 13.3 %term.1 = (bf16[16,8192]{1,0:T(8,128)(2,1)}, bf16[16,8192]{1,0:T(8,128)(2,1)}, bf16[16,8192]{1,0:T(8,128)(2,1)}, bf16[16,8192]{1,0:T(8,128)(2,1)}, bf16[16,8192]...) custom-call(s32[1]{0:T(128)} %bitcast.here_ref, ...), custom_call_target="tpu_custom_call" | custom-call | flops 12000000000 | tf_op jit(solution)/shard_map/term/pallas_call | solution.py:358
  173.9 1.6 collective-permute-start.6
  175.5 1.2 collective-permute-start.7
  176.7 2.2 collective-permute-start.8
  178.9 3.4 %collective-permute-start.1 = (bf16[16,8192]{1,0:T(8,128)(2,1)}, bf16[16,8192]{1,0:T(8,128)(2,1)S(1)}, u32[]{:S(2)}, u32[]{:S(2)}) collective-permute-start(bf16[16,8192]{1,0:T(8,128)(2,1)} %get-tuple-element.34), channel_id=1, source_target_pairs={{0,64},{32,96},{64,0},{96,32},{1,65},{33,97},{65,1},{97,33},{2,66}... | collective-permute-start | bytes 786440 | tf_op jit(solution)/shard_map/ppermute | solution.py:441
  182.3 5.4 %collective-permute-done.6.refs_1_ = bf16[16,8192]{1,0:T(8,128)(2,1)S(1)} collective-permute-done((bf16[16,8192]{1,0:T(8,128)(2,1)}, bf16[16,8192]{1,0:T(8,128)(2,1)S(1)}, u32[]{:S(2)}, u32[]{:S(2)}) %collective-permute-start.6) | collective-permute-done | bytes 262176 | tf_op jit(solution)/shard_map/ppermute | solution.py:441
  187.7 4.5 %collective-permute-done.8.refs_3_ = bf16[16,8192]{1,0:T(8,128)(2,1)S(1)} collective-permute-done((bf16[16,8192]{1,0:T(8,128)(2,1)}, bf16[16,8192]{1,0:T(8,128)(2,1)S(1)}, u32[]{:S(2)}, u32[]{:S(2)}) %collective-permute-start.8) | collective-permute-done | bytes 262176 | tf_op jit(solution)/shard_map/ppermute | solution.py:441
  192.1 0.9 copy-done.5
  193.1 1.4 suffix_sums.3
  194.5 1.2 collective-permute-start.10
  195.7 2.0 collective-permute-start.9
  197.7 9.3 %collective-permute-done.2.refs_3_ = bf16[16,8192]{1,0:T(8,128)(2,1)S(1)} collective-permute-done((bf16[16,8192]{1,0:T(8,128)(2,1)}, bf16[16,8192]{1,0:T(8,128)(2,1)S(1)}, u32[]{:S(2)}, u32[]{:S(2)}) %collective-permute-start.2) | collective-permute-done | bytes 262176 | tf_op jit(solution)/shard_map/ppermute | solution.py:441
  207.0 1.5 suffix_sums.2
  209.2 2.0 collective-permute-start.5
  211.2 1.9 unpack.1
  213.6 5.2 %collective-permute-done.3.refs_1_ = bf16[16,8192]{1,0:T(8,128)(2,1)} collective-permute-done((bf16[16,8192]{1,0:T(8,128)(2,1)}, bf16[16,8192]{1,0:T(8,128)(2,1)}, u32[]{:S(2)}, u32[]{:S(2)}) %collective-permute-start.3) | collective-permute-done | bytes 262176 | tf_op jit(solution)/shard_map/ppermute | solution.py:441
  218.8 6.1 %collective-permute-done.4.refs_2_ = bf16[16,8192]{1,0:T(8,128)(2,1)} collective-permute-done((bf16[16,8192]{1,0:T(8,128)(2,1)}, bf16[16,8192]{1,0:T(8,128)(2,1)}, u32[]{:S(2)}, u32[]{:S(2)}) %collective-permute-start.4) | collective-permute-done | bytes 262176 | tf_op jit(solution)/shard_map/ppermute | solution.py:441
  224.9 2.5 %place.1 = bf16[128,8192]{1,0:T(8,128)(2,1)} custom-call(s32[1]{0:T(128)} %bitcast.here_ref, bf16[16,8192]{1,0:T(8,128)(2,1)S(1)} %copy-done.3, bf16[16,8192]{1,0:T(8,128)(2,1)} %collective-permute-done.3.refs_1_, bf16[16,8192]{1,0:T(8,128)(2,1)} %collective-permute-done.4.refs_2_, bf16[16,8192]{1,0:T(8,128)(2,1)} %collective-permute-done.5.refs_3_, ...), custom_call_target="tpu_custom_call" | custom-call | flops 2000000000 | tf_op jit(solution)/shard_map/place/pallas_call | solution.py:423
  (30 shorter events, 2.8 us)
Async XLA Ops:
  7.2 153.5 %all-gather.3.cloned.1.call-start = ((), (), s32[]{:S(2)}) async-start(), calls=%async_computation.3 | async-start | bytes 17301504 | tf_op jit(solution)/shard_map/all_gather | solution.py:447
  119.7 32.7 %all-to-all-start.1 = ((bf16[32,64,128]{2,1,0:T(8,128)(2,1)}), bf16[32,64,128]{2,1,0:T(8,128)(2,1)S(1)}, u32[]{:S(2)}, u32[]{:S(2)}) async-start(bf16[32,64,128]{2,1,0:T(8,128)(2,1)} %bitcast.22), calls=%async_computation.1 | async-start | bytes 1048576 | tf_op jit(solution)/shard_map/all_to_all | solution.py:436
  152.4 0.8 copy-start.6
  153.1 58.1 %all-to-all-start.2 = ((bf16[32,64,640]{2,1,0:T(8,128)(2,1)}), bf16[32,64,640]{2,1,0:T(8,128)(2,1)S(1)}, u32[]{:S(2)}, u32[]{:S(2)}) async-start(bf16[32,64,640]{2,1,0:T(8,128)(2,1)} %bitcast.21), calls=%async_computation.2 | async-start | bytes 5242880 | tf_op jit(solution)/shard_map/all_to_all | solution.py:436
  173.9 13.7 %collective-permute-start.6 = (bf16[16,8192]{1,0:T(8,128)(2,1)}, bf16[16,8192]{1,0:T(8,128)(2,1)S(1)}, u32[]{:S(2)}, u32[]{:S(2)}) collective-permute-start(bf16[16,8192]{1,0:T(8,128)(2,1)} %get-tuple-element.41), channel_id=1, source_target_pairs={{0,32},{32,64},{64,96},{96,0},{1,33},{33,65},{65,97},{97,1},{2,34}... | collective-permute-start | bytes 786440 | tf_op jit(solution)/shard_map/ppermute | solution.py:441
  175.5 12.2 %collective-permute-start.7 = (bf16[16,8192]{1,0:T(8,128)(2,1)}, bf16[16,8192]{1,0:T(8,128)(2,1)S(1)}, u32[]{:S(2)}, u32[]{:S(2)}) collective-permute-start(bf16[16,8192]{1,0:T(8,128)(2,1)} %get-tuple-element.42), channel_id=1, source_target_pairs={{0,64},{32,96},{64,0},{96,32},{1,65},{33,97},{65,1},{97,33},{2,66}... | collective-permute-start | bytes 786440 | tf_op jit(solution)/shard_map/ppermute | solution.py:441
  176.7 15.5 %collective-permute-start.8 = (bf16[16,8192]{1,0:T(8,128)(2,1)}, bf16[16,8192]{1,0:T(8,128)(2,1)S(1)}, u32[]{:S(2)}, u32[]{:S(2)}) collective-permute-start(bf16[16,8192]{1,0:T(8,128)(2,1)} %get-tuple-element.43), channel_id=1, source_target_pairs={{0,96},{32,0},{64,32},{96,64},{1,97},{33,1},{65,33},{97,65},{2,98}... | collective-permute-start | bytes 786440 | tf_op jit(solution)/shard_map/ppermute | solution.py:441
  178.8 16.8 %collective-permute-start = (bf16[16,8192]{1,0:T(8,128)(2,1)}, bf16[16,8192]{1,0:T(8,128)(2,1)S(1)}, u32[]{:S(2)}, u32[]{:S(2)}) collective-permute-start(bf16[16,8192]{1,0:T(8,128)(2,1)} %get-tuple-element.33), channel_id=1, source_target_pairs={{0,32},{32,64},{64,96},{96,0},{1,33},{33,65},{65,97},{97,1},{2,34}... | collective-permute-start | bytes 786440 | tf_op jit(solution)/shard_map/ppermute | solution.py:441
  178.9 18.9 %collective-permute-start.1 = (bf16[16,8192]{1,0:T(8,128)(2,1)}, bf16[16,8192]{1,0:T(8,128)(2,1)S(1)}, u32[]{:S(2)}, u32[]{:S(2)}) collective-permute-start(bf16[16,8192]{1,0:T(8,128)(2,1)} %get-tuple-element.34), channel_id=1, source_target_pairs={{0,64},{32,96},{64,0},{96,32},{1,65},{33,97},{65,1},{97,33},{2,66}... | collective-permute-start | bytes 786440 | tf_op jit(solution)/shard_map/ppermute | solution.py:441
  187.7 19.3 %collective-permute-start.2 = (bf16[16,8192]{1,0:T(8,128)(2,1)}, bf16[16,8192]{1,0:T(8,128)(2,1)S(1)}, u32[]{:S(2)}, u32[]{:S(2)}) collective-permute-start(bf16[16,8192]{1,0:T(8,128)(2,1)} %get-tuple-element.35), channel_id=1, source_target_pairs={{0,96},{32,0},{64,32},{96,64},{1,97},{33,1},{65,33},{97,65},{2,98}... | collective-permute-start | bytes 786440 | tf_op jit(solution)/shard_map/ppermute | solution.py:441
  192.1 1.0 copy-start.5
  193.1 13.9 %copy-start.4 = (bf16[16,8192]{1,0:T(8,128)(2,1)S(1)}, bf16[16,8192]{1,0:T(8,128)(2,1)}, u32[]{:S(2)}) copy-start(bf16[16,8192]{1,0:T(8,128)(2,1)} %get-tuple-element.32.refs_0_) | copy-start | bytes 786436
  194.5 13.9 %copy-start = (bf16[16,8192]{1,0:T(8,128)(2,1)}, bf16[16,8192]{1,0:T(8,128)(2,1)S(1)}, u32[]{:S(2)}) copy-start(bf16[16,8192]{1,0:T(8,128)(2,1)S(1)} %get-tuple-element.44.refs_4_) | copy-start | bytes 786436
  194.5 14.7 %collective-permute-start.10 = (bf16[16,8192]{1,0:T(8,128)(2,1)S(1)}, bf16[16,8192]{1,0:T(8,128)(2,1)S(1)}, u32[]{:S(2)}, u32[]{:S(2)}) collective-permute-start(bf16[16,8192]{1,0:T(8,128)(2,1)S(1)} %get-tuple-element.46), channel_id=1, source_target_pairs={{0,64},{32,96},{64,0},{96,32},{1,65},{33,97},{65,1},{97,33},{2,66}... | collective-permute-start | bytes 786440 | tf_op jit(solution)/shard_map/ppermute | solution.py:441
  195.7 17.4 %collective-permute-start.11 = (bf16[16,8192]{1,0:T(8,128)(2,1)}, bf16[16,8192]{1,0:T(8,128)(2,1)S(1)}, u32[]{:S(2)}, u32[]{:S(2)}) collective-permute-start(bf16[16,8192]{1,0:T(8,128)(2,1)} %get-tuple-element.47), channel_id=1, source_target_pairs={{0,32},{32,64},{64,96},{96,0},{1,33},{33,65},{65,97},{97,1},{2,34}... | collective-permute-start | bytes 786440 | tf_op jit(solution)/shard_map/ppermute | solution.py:441
  195.7 17.9 %collective-permute-start.9 = (bf16[16,8192]{1,0:T(8,128)(2,1)}, bf16[16,8192]{1,0:T(8,128)(2,1)S(1)}, u32[]{:S(2)}, u32[]{:S(2)}) collective-permute-start(bf16[16,8192]{1,0:T(8,128)(2,1)} %get-tuple-element.45), channel_id=1, source_target_pairs={{0,96},{32,0},{64,32},{96,64},{1,97},{33,1},{65,33},{97,65},{2,98}... | collective-permute-start | bytes 786440 | tf_op jit(solution)/shard_map/ppermute | solution.py:441
  208.5 0.7 copy-start.2
  209.2 9.6 %collective-permute-start.3 = (bf16[16,8192]{1,0:T(8,128)(2,1)}, bf16[16,8192]{1,0:T(8,128)(2,1)}, u32[]{:S(2)}, u32[]{:S(2)}) collective-permute-start(bf16[16,8192]{1,0:T(8,128)(2,1)} %get-tuple-element.37), channel_id=1, source_target_pairs={{0,96},{32,0},{64,32},{96,64},{1,97},{33,1},{65,33},{97,65},{2,98}... | collective-permute-start | bytes 786440 | tf_op jit(solution)/shard_map/ppermute | solution.py:441
  209.2 15.7 %collective-permute-start.4 = (bf16[16,8192]{1,0:T(8,128)(2,1)}, bf16[16,8192]{1,0:T(8,128)(2,1)}, u32[]{:S(2)}, u32[]{:S(2)}) collective-permute-start(bf16[16,8192]{1,0:T(8,128)(2,1)} %get-tuple-element.38), channel_id=1, source_target_pairs={{0,64},{32,96},{64,0},{96,32},{1,65},{33,97},{65,1},{97,33},{2,66}... | collective-permute-start | bytes 786440 | tf_op jit(solution)/shard_map/ppermute | solution.py:441
  209.2 15.7 %collective-permute-start.5 = (bf16[16,8192]{1,0:T(8,128)(2,1)}, bf16[16,8192]{1,0:T(8,128)(2,1)}, u32[]{:S(2)}, u32[]{:S(2)}) collective-permute-start(bf16[16,8192]{1,0:T(8,128)(2,1)} %get-tuple-element.39), channel_id=1, source_target_pairs={{0,32},{32,64},{64,96},{96,0},{1,33},{33,65},{65,97},{97,1},{2,34}... | collective-permute-start | bytes 786440 | tf_op jit(solution)/shard_map/ppermute | solution.py:441
  211.2 13.7 %copy-start.1 = (bf16[16,8192]{1,0:T(8,128)(2,1)S(1)}, bf16[16,8192]{1,0:T(8,128)(2,1)}, u32[]{:S(2)}) copy-start(bf16[16,8192]{1,0:T(8,128)(2,1)} %copy-done) | copy-start | bytes 786436
  211.2 13.7 %copy-start.3 = (bf16[16,8192]{1,0:T(8,128)(2,1)S(1)}, bf16[16,8192]{1,0:T(8,128)(2,1)}, u32[]{:S(2)}) copy-start(bf16[16,8192]{1,0:T(8,128)(2,1)} %copy-done.2) | copy-start | bytes 786436
Sparse Core Ops, SparseCore 0:
  10.3 131.5 all-gather.2
